TPU v7x, 256 devices: a whole 4x4x8 slice. The times are simulated.
256 devices in a mesh: pipe: 8 (over z_lo, core), seq: 32 (over z_hi, y, x).
Axes of the slice: x: 4, y: 4, z: 8 (z_hi: 2, z_lo: 4; z = z_hi * 4 + z_lo), core: 2. Of those that a mesh axis runs over, the one named last changes fastest.
Arguments:
- queries: bfloat16 [8, 4096, 12288], P('pipe', 'seq'), may hold values from -6 to 6
- keys: bfloat16 [8, 4096, 12288], P('pipe', 'seq'), may hold values from -6 to 6
- values: bfloat16 [8, 4096, 8192], P('pipe', 'seq'), may hold values from -6 to 6
- doc_lengths: int32 [8, 16], replicated, may hold values from 1 to 512, 4096 in all within a row
Outputs:
- mtp_attention: bfloat16 [8, 4096, 8192], P('pipe', 'seq')
All inputs are finite; a program needn't handle non-finite values.
Results may differ from a plain program's by a relative error of at most 0.0046.
Values may be sent and summed in bfloat16 or wider, within the bound.
No kernel may reach another device: no remote copies, remote signals or barrier semaphores. Data moves between devices by JAX's collectives and lax.ppermute only.
A program may use at most 128 MiB of HBM per device.

v0:
```python
import functools
import jax
import jax.numpy as jnp
from jax import lax
from jax.experimental import pallas as pl
from jax.experimental.pallas import tpu as pltpu
from jax.sharding import PartitionSpec as P

HEADS = 64
DQK = 192
DV = 128
DOCS = 16
LONGEST = 512
BLOCK = 256
LANES = 128
EXTRA = (128, 256, 512)
CHUNKS = 2
SIDE = 4
GROUP = SIDE * SIDE
PER = HEADS // CHUNKS // GROUP
WQK = PER * DQK
WV = PER * DV
WKV = WQK + WV
NEGATIVE = -1e30
ANY = pl.BlockSpec(memory_space=pl.ANY)
SMEM = pl.BlockSpec(memory_space=pltpu.SMEM)


def run_copies(copies):
    for copy in copies:
        copy.start()
    for copy in copies:
        copy.wait()


def run_some(copies):
    for wanted, copy in copies:
        pl.when(wanted)(copy.start)
    for wanted, copy in copies:
        pl.when(wanted)(copy.wait)


def member_of(place, order, first, second, sign):
    ahead, aside = (second, first) if order == "xy" else (first, second)
    y = lax.rem(place[0] + SIDE + sign * ahead, SIDE)
    x = lax.rem(place[1] + SIDE + sign * aside, SIDE)
    return y * SIDE + x


def pack_kernel(plan, order, place, *refs):
    count = len(plan)
    sources, targets = refs[:count], refs[count : count + SIDE]
    buffer, in_sems, out_sems = refs[count + SIDE :]
    arriving, leaving = [], []
    for first in range(SIDE):
        group = []
        for second in range(SIDE):
            member = member_of(place, order, first, second, 1)
            for number, (source, (begin, width, at)) in enumerate(zip(sources, plan)):
                column = pl.multiple_of(begin + member * width, 128)
                group.append(
                    pltpu.make_async_copy(
                        source.at[0, :, pl.ds(column, width)],
                        buffer.at[first, second, :, pl.ds(at, width)],
                        in_sems.at[first, second, number],
                    )
                )
        arriving.append(group)
        leaving.append(pltpu.make_async_copy(buffer.at[first], targets[first], out_sems.at[first]))
    for group in arriving:
        for copy in group:
            copy.start()
    for first in range(SIDE):
        for copy in arriving[first]:
            copy.wait()
        leaving[first].start()
    for copy in leaving:
        copy.wait()


def pack(place, order, parts):
    rows = parts[0][0].shape[1]
    plan, at = [], 0
    for _, first, width in parts:
        plan.append((first, width, at))
        at += width
    return pl.pallas_call(
        functools.partial(pack_kernel, tuple(plan), order),
        out_shape=[jax.ShapeDtypeStruct((SIDE, rows, at), jnp.bfloat16)] * SIDE,
        in_specs=[SMEM] + [ANY] * len(parts),
        out_specs=[ANY] * SIDE,
        scratch_shapes=[
            pltpu.VMEM((SIDE, SIDE, rows, at), jnp.bfloat16),
            pltpu.SemaphoreType.DMA((SIDE, SIDE, len(parts))),
            pltpu.SemaphoreType.DMA((SIDE,)),
        ],
        name="pack",
    )(place, *[part[0] for part in parts])


def repack_kernel(begin, *refs):
    sources, targets = refs[:SIDE], refs[SIDE:-3]
    buffer, in_sems, out_sems = refs[-3:]
    count = SIDE - begin
    run_copies(
        [
            pltpu.make_async_copy(
                sources[first].at[pl.ds(begin, count)], buffer.at[:, first], in_sems.at[first]
            )
            for first in range(SIDE)
        ]
    )
    run_copies(
        [
            pltpu.make_async_copy(buffer.at[second], targets[second], out_sems.at[second])
            for second in range(count)
        ]
    )


def repack(arrays, begin):
    shape = arrays[0].shape
    count = SIDE - begin
    return pl.pallas_call(
        functools.partial(repack_kernel, begin),
        out_shape=[jax.ShapeDtypeStruct(shape, jnp.bfloat16)] * count,
        in_specs=[ANY] * SIDE,
        out_specs=[ANY] * count,
        scratch_shapes=[
            pltpu.VMEM((count,) + shape, jnp.bfloat16),
            pltpu.SemaphoreType.DMA((SIDE,)),
            pltpu.SemaphoreType.DMA((count,)),
        ],
        name="repack",
    )(*arrays)


def send(block, axis, distance, shifted=False):
    return routed(block, axis, distance, shifted)


def routed(block, axis, distance, shifted):
    routes = []
    for half in range(2):
        for y in range(SIDE):
            for x in range(SIDE):
                to_y = (y + distance) % SIDE if axis == "y" else y
                to_x = (x + distance) % SIDE if axis == "x" else x
                routes.append((half * GROUP + y * SIDE + x, half * GROUP + to_y * SIDE + to_x))
    if not shifted:
        return lax.ppermute(block, "seq", routes)
    segments, members = lax.axis_size("pipe"), lax.axis_size("seq")
    routes = [
        (segment * members + a, (segment + 1) % segments * members + b)
        for segment in range(segments)
        for a, b in routes
    ]
    return lax.ppermute(block, ("pipe", "seq"), routes)


def shift(block):
    segments = lax.axis_size("pipe")
    return lax.ppermute(block, "pipe", [(i, (i + 1) % segments) for i in range(segments)])


def first_stage(arrays, order, shifted=False):
    if shifted:
        return [send(array, order[0], i, True) for i, array in enumerate(arrays)]
    return [arrays[0]] + [send(arrays[i], order[0], i) for i in range(1, SIDE)]


def second_stage(arrays, order):
    got = [send(array, order[1], i + 1) for i, array in enumerate(repack(arrays, 1))]
    got = list(arrays) + got
    table = {}
    for first in range(SIDE):
        for second in range(SIDE):
            key = (second, first) if order == "xy" else (first, second)
            if second == 0:
                table[key] = (first, 0)
            else:
                table[key] = (SIDE + second - 1, first)
    return got, table


def edge_kernel(table, place, *refs):
    sources, (target, buffer, sems) = refs[:-3], refs[-3:]
    last = lax.rem(place[0] + 1, SIDE)
    for ahead in range(SIDE):

        @pl.when(last == ahead)
        def _():
            copies = []
            for aside in range(SIDE):
                array, at = table[(ahead, aside)]
                copies.append(
                    pltpu.make_async_copy(sources[array].at[at], buffer.at[aside], sems.at[aside])
                )
            run_copies(copies)

    run_copies([pltpu.make_async_copy(buffer, target, sems.at[0])])


def send_edge(place, arrays, table):
    shape = arrays[0].shape
    edge = pl.pallas_call(
        functools.partial(edge_kernel, table),
        out_shape=jax.ShapeDtypeStruct(shape, jnp.bfloat16),
        in_specs=[SMEM] + [ANY] * len(arrays),
        out_specs=ANY,
        scratch_shapes=[pltpu.VMEM(shape, jnp.bfloat16), pltpu.SemaphoreType.DMA((SIDE,))],
        name="edge",
    )(place, *arrays)
    return lax.ppermute(edge, "seq", [(i, i + GROUP) for i in range(GROUP)])


def place_kernel(first, table, place, *refs):
    target, buffer, in_sems, out_sem = refs[-4:]
    width = refs[0].shape[2]
    pieces = refs
    copies = []
    if table is None:
        table = {(0, at): (0, at) for at in range(GROUP)}
    for (ahead, aside), (array, at) in table.items():
        member = aside
        if pieces[0].shape[0] != GROUP:
            member = member_of(place, "yx", ahead, aside, -1)
        column = pl.multiple_of(member * width, 128)
        copies.append(
            pltpu.make_async_copy(
                pieces[array].at[at], buffer.at[:, pl.ds(column, width)], in_sems.at[array, at]
            )
        )
    run_copies(copies)
    run_copies(
        [pltpu.make_async_copy(buffer, target.at[0, :, pl.ds(first, GROUP * width)], out_sem.at[0])]
    )


def put(place, arrays, table, first, columns, whole=None):
    _, rows, width = arrays[0].shape
    extra = [] if whole is None else [whole]
    return pl.pallas_call(
        functools.partial(place_kernel, first, table),
        out_shape=jax.ShapeDtypeStruct((1, rows, columns), jnp.bfloat16),
        in_specs=[SMEM] + [ANY] * (len(arrays) + len(extra)),
        out_specs=ANY,
        scratch_shapes=[
            pltpu.VMEM((rows, GROUP * width), jnp.bfloat16),
            pltpu.SemaphoreType.DMA((len(arrays), GROUP)),
            pltpu.SemaphoreType.DMA((1,)),
        ],
        input_output_aliases={len(arrays) + 1: 0} if extra else {},
        name="place",
    )(place, *arrays, *extra)


def latest_start(doc_starts, position):
    start = jnp.zeros_like(position)
    for doc in range(1, DOCS):
        start = jnp.where(position >= doc_starts[doc], doc_starts[doc], start)
    return start


def attend(doc_starts, first_position, queries_in, window, mixed_out, first, last):
    lane = lax.broadcasted_iota(jnp.int32, (BLOCK, LANES), 1)
    sublane = lax.broadcasted_iota(jnp.int32, (BLOCK, LANES), 0)
    column = lax.broadcasted_iota(jnp.int32, (BLOCK, 2 * LANES), 1)
    scale = DQK ** (-0.5)

    def heads(row, start, span):
        above = LONGEST + BLOCK - span
        begin = pl.multiple_of(row + above, LANES)
        start = start - (first_position + row - LONGEST + above)
        masks = []
        for part in range(span // LANES):
            visible = lane + part * LANES >= start
            if part * LANES >= span - BLOCK:
                visible = visible & (lane + (part * LANES - (span - BLOCK)) <= sublane)
            masks.append(visible)
        mask = jnp.concatenate(masks, axis=1)
        scores, values = [], []
        for head in range(PER):
            columns = slice(LANES * head, LANES * head + 2 * LANES)
            query = queries_in[pl.ds(row, BLOCK), columns]
            inside = column < DQK if head == 0 else column >= 2 * LANES - DQK
            query = jnp.where(inside, query, jnp.zeros_like(query))
            scores.append(
                lax.dot_general(
                    query,
                    window[pl.ds(begin, span), columns],
                    (((1,), (1,)), ((), ())),
                    preferred_element_type=jnp.float32,
                )
            )
            values.append(window[pl.ds(begin, span), WQK + DV * head : WQK + DV * (head + 1)])
        scores = [jnp.where(mask, score, NEGATIVE) for score in scores]
        tops = [jnp.max(score, axis=1, keepdims=True) for score in scores]
        exponents = [jnp.exp((score - top) * scale) for score, top in zip(scores, tops)]
        totals = [jnp.sum(exponent, axis=1, keepdims=True) for exponent in exponents]
        weights = [
            (exponent * (1.0 / total)).astype(jnp.bfloat16)
            for exponent, total in zip(exponents, totals)
        ]
        for head in range(PER):
            mixed = jnp.dot(weights[head], values[head], preferred_element_type=jnp.float32)
            mixed_out[pl.ds(row, BLOCK), DV * head : DV * (head + 1)] = mixed.astype(jnp.bfloat16)

    def block(number, carry):
        row = pl.multiple_of(number * BLOCK, BLOCK)
        position = first_position + row
        start = latest_start(doc_starts, position + sublane)
        back = position - latest_start(doc_starts, position)
        shorter = 0
        for extra in EXTRA:
            pl.when((back > shorter) & (back <= extra) | (back == 0) & (shorter == 0))(
                functools.partial(heads, row, start, BLOCK + extra)
            )
            shorter = extra
        return carry

    lax.fori_loop(first, last, block, 0)


def attention_kernel(plan, doc_starts, place, *refs):
    query_table, key_table, order, query_count, key_count, part = plan
    queries, keys = refs[:query_count], refs[query_count : query_count + key_count]
    edge = refs[query_count + key_count]
    queries_in, window, mixed_out, sems, edge_sems = refs[-5:]
    targets = refs[-5 - (1 if order is None else SIDE) : -5]
    rows = queries_in.shape[0]
    block_rows = rows // GROUP
    copies = []
    for (ahead, aside), (array, at) in query_table.items():
        member = member_of(place, "yx", ahead, aside, -1)
        row = pl.multiple_of(member * block_rows, block_rows)
        top = member < SIDE
        query_wanted = {"all": True, "rest": ~top, "edge": top}[part]
        key_wanted = {"all": True, "rest": True, "edge": top}[part]
        copies.append(
            (
                query_wanted,
                pltpu.make_async_copy(
                    queries[array].at[at],
                    queries_in.at[pl.ds(row, block_rows)],
                    sems.at[0, ahead, aside],
                ),
            )
        )
        array, at = key_table[(ahead, aside)]
        copies.append(
            (
                key_wanted,
                pltpu.make_async_copy(
                    keys[array].at[at],
                    window.at[pl.ds(LONGEST + row, block_rows)],
                    sems.at[1, ahead, aside],
                ),
            )
        )
    if part != "rest":
        for aside in range(SIDE):
            row = pl.multiple_of(lax.rem(place[1] + SIDE - aside, SIDE) * block_rows, block_rows)
            copies.append(
                (
                    True,
                    pltpu.make_async_copy(
                        edge.at[aside], window.at[pl.ds(row, block_rows)], edge_sems.at[aside]
                    ),
                )
            )
    run_some(copies)
    border = LONGEST // BLOCK
    first = border if part == "rest" else 0
    last = border if part == "edge" else rows // BLOCK
    attend(doc_starts, place[2], queries_in, window, mixed_out, first, last)
    if order is None:
        run_copies([pltpu.make_async_copy(mixed_out, targets[0], edge_sems.at[0])])
        return
    copies = []
    for first in range(SIDE):
        for second in range(SIDE):
            member = member_of(place, order, first, second, 1)
            row = pl.multiple_of(member * block_rows, block_rows)
            top = member < SIDE
            copies.append(
                (
                    {"all": True, "rest": ~top, "edge": top}[part],
                    pltpu.make_async_copy(
                        mixed_out.at[pl.ds(row, block_rows)],
                        targets[first].at[second],
                        sems.at[0, first, second],
                    ),
                )
            )
    run_some(copies)


def attention(doc_starts, place, query, key_value, edge, order, part="all", whole=()):
    (queries, query_table), (keys, key_table) = query, key_value
    block_rows = keys[0].shape[1]
    rows = GROUP * block_rows
    plan = (query_table, key_table, order, len(queries), len(keys), part)
    outs = [(rows, WV)] if order is None else [(SIDE, block_rows, WV)] * SIDE
    operands = [doc_starts, place, *queries, *keys, edge]
    return pl.pallas_call(
        functools.partial(attention_kernel, plan),
        out_shape=[jax.ShapeDtypeStruct(shape, jnp.bfloat16) for shape in outs],
        in_specs=[SMEM, SMEM] + [ANY] * (len(operands) + len(whole) - 2),
        out_specs=[ANY] * len(outs),
        scratch_shapes=[
            pltpu.VMEM((rows, WQK), jnp.bfloat16),
            pltpu.VMEM((LONGEST + rows, WKV), jnp.bfloat16),
            pltpu.VMEM((rows, WV), jnp.bfloat16),
            pltpu.SemaphoreType.DMA((2, SIDE, SIDE)),
            pltpu.SemaphoreType.DMA((SIDE,)),
        ],
        input_output_aliases={len(operands) + i: i for i in range(len(whole))},
        name="attention",
    )(*operands, *whole)


def exchange(block):
    groups = [[half * GROUP + i for i in range(GROUP)] for half in range(2)]
    return lax.all_to_all(
        block, "seq", split_axis=0, concat_axis=0, axis_index_groups=groups, tiled=True
    )


def together(*arrays):
    return lax.optimization_barrier(arrays)


def local(queries, keys, values, doc_lengths):
    segment = lax.axis_index("pipe")
    segments = lax.axis_size("pipe")
    seq = lax.axis_index("seq")
    doc_starts = jnp.cumsum(doc_lengths, axis=1) - doc_lengths
    starts_here = lax.dynamic_index_in_dim(doc_starts, segment, 0, keepdims=False)
    starts_before = lax.dynamic_index_in_dim(
        doc_starts, (segment + segments - 1) % segments, 0, keepdims=False
    )
    rows = queries.shape[1]
    half, member = seq // GROUP, seq % GROUP
    place = jnp.stack([member // SIDE, member % SIDE, half * (GROUP * rows)]).astype(jnp.int32)
    columns = HEADS * DV
    second_qk, second_v = HEADS * DQK // 2, HEADS * DV // 2

    kv_first = pack(place, "xy", [(keys, 0, WQK), (values, 0, WV)])
    kv_first = first_stage(kv_first, "xy")
    kv_second = pack(place, "yx", [(keys, second_qk, WQK), (values, second_v, WV)])
    kv_second = first_stage(kv_second, "yx", True)
    q_second = shift(queries[:, :, second_qk:])
    queries, kv_first[1] = together(queries, kv_first[1])
    q_first = list(pack(place, "xy", [(queries, 0, WQK)]))
    kv_first[3], q_first[1] = together(kv_first[3], q_first[1])
    q_first = first_stage(q_first, "xy")
    q_second = first_stage(pack(place, "yx", [(q_second, 0, WQK)]), "yx")

    kv_first = second_stage(kv_first, "xy")
    kv_second = second_stage(kv_second, "yx")
    edge_first = send_edge(place, *kv_first)
    q_first = second_stage(q_first, "xy")
    edge_second = send_edge(place, *kv_second)
    q_second = second_stage(q_second, "yx")

    (out,) = attention(starts_here, place, q_first, kv_first, edge_first, None)
    out_first = exchange(out.reshape(GROUP, rows, WV))
    second = (starts_before, place, q_second, kv_second)
    out = attention(*second, kv_second[0][0], "yx", "rest")
    out = attention(*second, edge_second, "yx", "edge", tuple(out))
    out, table = second_stage(first_stage(out, "yx"), "yx")
    out_first = shift(out_first)
    whole = put(place, [out_first], None, 0, columns)
    return put(place, out, table, second_v, columns, whole)


def solution(mesh):
    placed = (P("pipe", "seq", None), P("pipe", "seq", None), P("pipe", "seq", None), P())
    return jax.shard_map(
        local, mesh=mesh, in_specs=placed, out_specs=P("pipe", "seq", None), check_vma=False
    )
```

profile of v0, /device:TPU:32, one launch (start us, length us, event | category | flops | bytes accessed | tf_op | source)
XLA Modules:
  0.0 311.7 jit_solution(4159023247568403101)
XLA Ops:
  0.7 3.6 %pack.6 = (bf16[4,128,640]{2,1,0:T(8,128)(2,1)}, bf16[4,128,640]{2,1,0:T(8,128)(2,1)}, bf16[4,128,640]{2,1,0:T(8,128)(2,1)}, bf16[4,128,640]{2,1,0:T(8,128)(2,1)}) custom-call(s32[3]{0:T(128)} %pad_add_fusion.place, bf16[1,128,12288]{2,1,0:T(8,128)(2,1)} %refs_0_.3, bf16[1,128,8192]{2,1,0:T(8,128)(2,1)} %refs_1_.3), custom_call_target="tpu_custom_call" | custom-call | tf_op jit(solution)/shard_map/pack/pallas_call | solution.py:87
  9.4 13.0 %collective-permute-done.21.refs_1_.refs_8_ = bf16[4,128,640]{2,1,0:T(8,128)(2,1)S(1)} collective-permute-done((bf16[4,128,640]{2,1,0:T(8,128)(2,1)}, bf16[4,128,640]{2,1,0:T(8,128)(2,1)S(1)}, u32[]{:S(2)}, u32[]{:S(2)}) %collective-permute-start.21) | collective-permute-done | bytes 655392 | tf_op jit(solution)/shard_map/ppermute | solution.py:151
  22.4 3.1 %pack.7 = (bf16[4,128,384]{2,1,0:T(8,128)(2,1)}, bf16[4,128,384]{2,1,0:T(8,128)(2,1)}, bf16[4,128,384]{2,1,0:T(8,128)(2,1)}, bf16[4,128,384]{2,1,0:T(8,128)(2,1)}) custom-call(s32[3]{0:T(128)} %pad_add_fusion.place, bf16[1,128,12288]{2,1,0:T(8,128)(2,1)} %refs_0_.4), custom_call_target="tpu_custom_call" | custom-call | tf_op jit(solution)/shard_map/pack/pallas_call | solution.py:87
  25.5 10.2 %collective-permute-done.22.refs_3_.refs_10_ = bf16[4,128,640]{2,1,0:T(8,128)(2,1)S(1)} collective-permute-done((bf16[4,128,640]{2,1,0:T(8,128)(2,1)}, bf16[4,128,640]{2,1,0:T(8,128)(2,1)S(1)}, u32[]{:S(2)}, u32[]{:S(2)}) %collective-permute-start.22) | collective-permute-done | bytes 655392 | tf_op jit(solution)/shard_map/ppermute | solution.py:151
  50.6 8.4 %collective-permute-done.30.refs_4_.refs_11_ = bf16[4,128,640]{2,1,0:T(8,128)(2,1)S(1)} collective-permute-done((bf16[4,128,640]{2,1,0:T(8,128)(2,1)}, bf16[4,128,640]{2,1,0:T(8,128)(2,1)S(1)}, u32[]{:S(2)}, u32[]{:S(2)}) %collective-permute-start.30) | collective-permute-done | bytes 655392 | tf_op jit(solution)/shard_map/ppermute | solution.py:151
  61.2 12.2 %collective-permute-done.31.refs_5_.refs_12_ = bf16[4,128,640]{2,1,0:T(8,128)(2,1)S(1)} collective-permute-done((bf16[4,128,640]{2,1,0:T(8,128)(2,1)}, bf16[4,128,640]{2,1,0:T(8,128)(2,1)S(1)}, u32[]{:S(2)}, u32[]{:S(2)}) %collective-permute-start.31) | collective-permute-done | bytes 655392 | tf_op jit(solution)/shard_map/ppermute | solution.py:151
  77.3 9.1 %collective-permute-start.33 = (bf16[4,128,640]{2,1,0:T(8,128)(2,1)}, bf16[4,128,640]{2,1,0:T(8,128)(2,1)}, u32[]{:S(2)}, u32[]{:S(2)}) collective-permute-start(bf16[4,128,640]{2,1,0:T(8,128)(2,1)} %edge.3), channel_id=1, source_target_pairs={{0,16},{1,17},{2,18},{3,19},{4,20},{5,21},{6,22},{7,23},{8,24},{9,... | collective-permute-start | bytes 1966088 | tf_op jit(solution)/shard_map/ppermute | solution.py:214
  95.6 3.8 %pack.5 = (bf16[4,128,640]{2,1,0:T(8,128)(2,1)}, bf16[4,128,640]{2,1,0:T(8,128)(2,1)}, bf16[4,128,640]{2,1,0:T(8,128)(2,1)}, bf16[4,128,640]{2,1,0:T(8,128)(2,1)}) custom-call(s32[3]{0:T(128)} %pad_add_fusion.place, bf16[1,128,12288]{2,1,0:T(8,128)(2,1)} %refs_0_.3, bf16[1,128,8192]{2,1,0:T(8,128)(2,1)} %refs_1_.3), custom_call_target="tpu_custom_call" | custom-call | tf_op jit(solution)/shard_map/pack/pallas_call | solution.py:87
  101.2 8.7 %collective-permute-done.27.refs_5_ = bf16[4,128,384]{2,1,0:T(8,128)(2,1)} collective-permute-done((bf16[4,128,384]{2,1,0:T(8,128)(2,1)}, bf16[4,128,384]{2,1,0:T(8,128)(2,1)}, u32[]{:S(2)}, u32[]{:S(2)}) %collective-permute-start.27) | collective-permute-done | bytes 393248 | tf_op jit(solution)/shard_map/ppermute | solution.py:151
  109.8 47.2 %collective-permute-done.33.refs_14_ = bf16[4,128,640]{2,1,0:T(8,128)(2,1)} collective-permute-done((bf16[4,128,640]{2,1,0:T(8,128)(2,1)}, bf16[4,128,640]{2,1,0:T(8,128)(2,1)}, u32[]{:S(2)}, u32[]{:S(2)}) %collective-permute-start.33) | collective-permute-done | bytes 655392 | tf_op jit(solution)/shard_map/ppermute | solution.py:214
  159.8 12.8 %attention.5 = bf16[2048,256]{1,0:T(8,128)(2,1)} custom-call(s32[16]{0:T(128)} %get-tuple-element.91.doc_starts, s32[3]{0:T(128)} %pad_add_fusion.place, bf16[4,128,384]{2,1,0:T(8,128)(2,1)} %get-tuple-element.75.refs_0_, bf16[4,128,384]{2,1,0:T(8,128)(2,1)} %copy-done.19, bf16[4,128,384]{2,1,0:T(8,128)(2,1)} %collective-permute-done.24.refs_2_, ...), custom_call_target="tpu_custom_call" | custom-call | tf_op jit(solution)/shard_map/attention/pallas_call | solution.py:406
  172.6 4.4 %all-to-all-start = ((bf16[16,128,256]{2,1,0:T(8,128)(2,1)}), bf16[16,128,256]{2,1,0:T(8,128)(2,1)}, u32[]{:S(2)}, u32[]{:S(2)}) async-start(bf16[16,128,256]{2,1,0:T(8,128)(2,1)} %bitcast.8), calls=%async_computation | async-start | bytes 2097152 | tf_op jit(solution)/shard_map/all_to_all | solution.py:425
  188.0 3.1 %pack.4 = (bf16[4,128,384]{2,1,0:T(8,128)(2,1)}, bf16[4,128,384]{2,1,0:T(8,128)(2,1)}, bf16[4,128,384]{2,1,0:T(8,128)(2,1)}, bf16[4,128,384]{2,1,0:T(8,128)(2,1)}) custom-call(s32[3]{0:T(128)} %pad_add_fusion.place, bf16[1,128,6144]{2,1,0:T(8,128)(2,1)} %collective-permute-done.refs_0_), custom_call_target="tpu_custom_call" | custom-call | tf_op jit(solution)/shard_map/pack/pallas_call | solution.py:87
  195.4 11.2 %collective-permute-done.11.refs_4_.refs_11_ = bf16[4,128,640]{2,1,0:T(8,128)(2,1)S(1)} collective-permute-done((bf16[4,128,640]{2,1,0:T(8,128)(2,1)}, bf16[4,128,640]{2,1,0:T(8,128)(2,1)S(1)}, u32[]{:S(2)}, u32[]{:S(2)}) %collective-permute-start.11) | collective-permute-done | bytes 655392 | tf_op jit(solution)/shard_map/ppermute | solution.py:151
  209.3 8.9 %collective-permute-done.12.refs_5_.refs_12_ = bf16[4,128,640]{2,1,0:T(8,128)(2,1)S(1)} collective-permute-done((bf16[4,128,640]{2,1,0:T(8,128)(2,1)}, bf16[4,128,640]{2,1,0:T(8,128)(2,1)S(1)}, u32[]{:S(2)}, u32[]{:S(2)}) %collective-permute-start.12) | collective-permute-done | bytes 655392 | tf_op jit(solution)/shard_map/ppermute | solution.py:151
  222.8 8.7 %collective-permute-start.14 = (bf16[4,128,640]{2,1,0:T(8,128)(2,1)}, bf16[4,128,640]{2,1,0:T(8,128)(2,1)S(1)}, u32[]{:S(2)}, u32[]{:S(2)}) collective-permute-start(bf16[4,128,640]{2,1,0:T(8,128)(2,1)} %edge.2), channel_id=1, source_target_pairs={{0,16},{1,17},{2,18},{3,19},{4,20},{5,21},{6,22},{7,23},{8,24},{9,... | collective-permute-start | bytes 1966088 | tf_op jit(solution)/shard_map/ppermute | solution.py:214
  238.3 15.2 %collective-permute-done.4.refs_4_ = bf16[4,128,384]{2,1,0:T(8,128)(2,1)S(1)} collective-permute-done((bf16[4,128,384]{2,1,0:T(8,128)(2,1)}, bf16[4,128,384]{2,1,0:T(8,128)(2,1)S(1)}, u32[]{:S(2)}, u32[]{:S(2)}) %collective-permute-start.4) | collective-permute-done | bytes 393248 | tf_op jit(solution)/shard_map/ppermute | solution.py:151
  254.9 10.1 %attention.3 = (bf16[4,128,256]{2,1,0:T(8,128)(2,1)}, bf16[4,128,256]{2,1,0:T(8,128)(2,1)}, bf16[4,128,256]{2,1,0:T(8,128)(2,1)}, bf16[4,128,256]{2,1,0:T(8,128)(2,1)}) custom-call(s32[16]{0:T(128)} %get-tuple-element.92.doc_starts, s32[3]{0:T(128)} %pad_add_fusion.place, bf16[4,128,384]{2,1,0:T(8,128)(2,1)} %get-tuple-element.48.refs_0_, ...), custom_call_target="tpu_custom_call" | custom-call | tf_op jit(solution)/shard_map/attention/pallas_call | solution.py:406
  265.9 5.0 %attention.4 = (bf16[4,128,256]{2,1,0:T(8,128)(2,1)}, bf16[4,128,256]{2,1,0:T(8,128)(2,1)}, bf16[4,128,256]{2,1,0:T(8,128)(2,1)}, bf16[4,128,256]{2,1,0:T(8,128)(2,1)}) custom-call(s32[16]{0:T(128)} %get-tuple-element.92.doc_starts, s32[3]{0:T(128)} %pad_add_fusion.place, ...), custom_call_target="tpu_custom_call", output_to_operand_aliasing={{0}: (17, {}), {1}: (18, {}), {2}: (19, {}), {3}: (20, {})} | custom-call | tf_op jit(solution)/shard_map/attention/pallas_call | solution.py:406
  276.6 3.7 %collective-permute-done.15.refs_1_ = bf16[4,128,256]{2,1,0:T(8,128)(2,1)S(1)} collective-permute-done((bf16[4,128,256]{2,1,0:T(8,128)(2,1)}, bf16[4,128,256]{2,1,0:T(8,128)(2,1)S(1)}, u32[]{:S(2)}, u32[]{:S(2)}) %collective-permute-start.15) | collective-permute-done | bytes 262176 | tf_op jit(solution)/shard_map/ppermute | solution.py:151
  280.3 6.3 %collective-permute-done.16.refs_2_ = bf16[4,128,256]{2,1,0:T(8,128)(2,1)S(1)} collective-permute-done((bf16[4,128,256]{2,1,0:T(8,128)(2,1)}, bf16[4,128,256]{2,1,0:T(8,128)(2,1)S(1)}, u32[]{:S(2)}, u32[]{:S(2)}) %collective-permute-start.16) | collective-permute-done | bytes 262176 | tf_op jit(solution)/shard_map/ppermute | solution.py:151
  291.2 3.5 %collective-permute-start.19 = (bf16[4,128,256]{2,1,0:T(8,128)(2,1)}, bf16[4,128,256]{2,1,0:T(8,128)(2,1)S(1)}, u32[]{:S(2)}, u32[]{:S(2)}) collective-permute-start(bf16[4,128,256]{2,1,0:T(8,128)(2,1)} %get-tuple-element.71), channel_id=1, source_target_pairs={{0,2},{1,3},{2,0},{3,1},{4,6},{5,7},{6,4},{7,5},{8,10},{9,11},{10,... | collective-permute-start | bytes 786440 | tf_op jit(solution)/shard_map/ppermute | solution.py:151
  299.7 6.6 %collective-permute-done.19.refs_5_ = bf16[4,128,256]{2,1,0:T(8,128)(2,1)S(1)} collective-permute-done((bf16[4,128,256]{2,1,0:T(8,128)(2,1)}, bf16[4,128,256]{2,1,0:T(8,128)(2,1)S(1)}, u32[]{:S(2)}, u32[]{:S(2)}) %collective-permute-start.19) | collective-permute-done | bytes 262176 | tf_op jit(solution)/shard_map/ppermute | solution.py:151
  307.7 3.9 %place.3 = bf16[1,128,8192]{2,1,0:T(8,128)(2,1)} custom-call(s32[3]{0:T(128)} %pad_add_fusion.place, bf16[4,128,256]{2,1,0:T(8,128)(2,1)} %get-tuple-element.66.refs_0_, bf16[4,128,256]{2,1,0:T(8,128)(2,1)} %copy-done.20, bf16[4,128,256]{2,1,0:T(8,128)(2,1)} %copy-done.21, bf16[4,128,256]{2,1,0:T(8,128)(2,1)} %copy-done.22, ...), custom_call_target="tpu_custom_call", output_to_operand_aliasing={{}: (8, {})} | custom-call | tf_op jit(solution)/shard_map/place/pallas_call | solution.py:243
  (127 shorter events, 88.6 us)
Async XLA Ops:
  5.9 29.8 %collective-permute-start.22 = (bf16[4,128,640]{2,1,0:T(8,128)(2,1)}, bf16[4,128,640]{2,1,0:T(8,128)(2,1)S(1)}, u32[]{:S(2)}, u32[]{:S(2)}) collective-permute-start(bf16[4,128,640]{2,1,0:T(8,128)(2,1)} %get-tuple-element.76), channel_id=1, source_target_pairs={{0,3},{1,0},{2,1},{3,2},{4,7},{5,4},{6,5},{7,6},{8,11},{9,8},{10,9... | collective-permute-start | bytes 1966088 | tf_op jit(solution)/shard_map/ppermute | solution.py:151
  7.6 29.7 %collective-permute-start.29 = (bf16[4,128,640]{2,1,0:T(8,128)(2,1)}, bf16[4,128,640]{2,1,0:T(8,128)(2,1)S(1)}, u32[]{:S(2)}, u32[]{:S(2)}) collective-permute-start(bf16[4,128,640]{2,1,0:T(8,128)(2,1)} %get-tuple-element.86), channel_id=1, source_target_pairs={{0,2},{1,3},{2,0},{3,1},{4,6},{5,7},{6,4},{7,5},{8,10},{9,11},{10,... | collective-permute-start | bytes 1966088 | tf_op jit(solution)/shard_map/ppermute | solution.py:151
  42.6 30.7 %collective-permute-start.31 = (bf16[4,128,640]{2,1,0:T(8,128)(2,1)}, bf16[4,128,640]{2,1,0:T(8,128)(2,1)S(1)}, u32[]{:S(2)}, u32[]{:S(2)}) collective-permute-start(bf16[4,128,640]{2,1,0:T(8,128)(2,1)} %get-tuple-element.89), channel_id=1, source_target_pairs={{0,8},{1,9},{2,10},{3,11},{4,12},{5,13},{6,14},{7,15},{8,0},{9,1},... | collective-permute-start | bytes 1966088 | tf_op jit(solution)/shard_map/ppermute | solution.py:151
  45.5 28.8 %collective-permute-start.32 = (bf16[4,128,640]{2,1,0:T(8,128)(2,1)}, bf16[4,128,640]{2,1,0:T(8,128)(2,1)}, u32[]{:S(2)}, u32[]{:S(2)}) collective-permute-start(bf16[4,128,640]{2,1,0:T(8,128)(2,1)} %get-tuple-element.90), channel_id=1, source_target_pairs={{0,12},{1,13},{2,14},{3,15},{4,0},{5,1},{6,2},{7,3},{8,4},{9,5},{1... | collective-permute-start | bytes 1966088 | tf_op jit(solution)/shard_map/ppermute | solution.py:151
  46.9 39.5 %collective-permute-start.23 = (bf16[4,128,384]{2,1,0:T(8,128)(2,1)}, bf16[4,128,384]{2,1,0:T(8,128)(2,1)S(1)}, u32[]{:S(2)}, u32[]{:S(2)}) collective-permute-start(bf16[4,128,384]{2,1,0:T(8,128)(2,1)} %get-tuple-element.78), channel_id=1, source_target_pairs={{0,1},{1,2},{2,3},{3,0},{4,5},{5,6},{6,7},{7,4},{8,9},{9,10},{10,1... | collective-permute-start | bytes 1179656 | tf_op jit(solution)/shard_map/ppermute | solution.py:151
  48.0 38.4 %collective-permute-start.24 = (bf16[4,128,384]{2,1,0:T(8,128)(2,1)}, bf16[4,128,384]{2,1,0:T(8,128)(2,1)}, u32[]{:S(2)}, u32[]{:S(2)}) collective-permute-start(bf16[4,128,384]{2,1,0:T(8,128)(2,1)} %get-tuple-element.79), channel_id=1, source_target_pairs={{0,2},{1,3},{2,0},{3,1},{4,6},{5,7},{6,4},{7,5},{8,10},{9,11},{10,... | collective-permute-start | bytes 1179656 | tf_op jit(solution)/shard_map/ppermute | solution.py:151
  58.9 27.5 %collective-permute-start.25 = (bf16[4,128,384]{2,1,0:T(8,128)(2,1)}, bf16[4,128,384]{2,1,0:T(8,128)(2,1)}, u32[]{:S(2)}, u32[]{:S(2)}) collective-permute-start(bf16[4,128,384]{2,1,0:T(8,128)(2,1)} %get-tuple-element.80), channel_id=1, source_target_pairs={{0,3},{1,0},{2,1},{3,2},{4,7},{5,4},{6,5},{7,6},{8,11},{9,8},{10,9... | collective-permute-start | bytes 1179656 | tf_op jit(solution)/shard_map/ppermute | solution.py:151
  77.3 79.8 %collective-permute-start.33 = (bf16[4,128,640]{2,1,0:T(8,128)(2,1)}, bf16[4,128,640]{2,1,0:T(8,128)(2,1)}, u32[]{:S(2)}, u32[]{:S(2)}) collective-permute-start(bf16[4,128,640]{2,1,0:T(8,128)(2,1)} %edge.3), channel_id=1, source_target_pairs={{0,16},{1,17},{2,18},{3,19},{4,20},{5,21},{6,22},{7,23},{8,24},{9,... | collective-permute-start | bytes 1966088 | tf_op jit(solution)/shard_map/ppermute | solution.py:214
  90.0 19.9 %collective-permute-start.27 = (bf16[4,128,384]{2,1,0:T(8,128)(2,1)}, bf16[4,128,384]{2,1,0:T(8,128)(2,1)}, u32[]{:S(2)}, u32[]{:S(2)}) collective-permute-start(bf16[4,128,384]{2,1,0:T(8,128)(2,1)} %get-tuple-element.82), channel_id=1, source_target_pairs={{0,8},{1,9},{2,10},{3,11},{4,12},{5,13},{6,14},{7,15},{8,0},{9,1},... | collective-permute-start | bytes 1179656 | tf_op jit(solution)/shard_map/ppermute | solution.py:151
  95.6 92.4 %collective-permute-start = (bf16[1,128,6144]{2,1,0:T(8,128)(2,1)}, bf16[1,128,6144]{2,1,0:T(8,128)(2,1)}, u32[]{:S(2)}, u32[]{:S(2)}) collective-permute-start(bf16[1,128,6144]{2,1,0:T(8,128)(2,1)} %slice.3), channel_id=1, source_target_pairs={{0,32},{32,64},{64,96},{96,128},{128,160},{160,192},{192,224},{224... | collective-permute-start | bytes 4718600 | tf_op jit(solution)/shard_map/ppermute | solution.py:163
  100.9 76.0 %collective-permute-start.7 = (bf16[4,128,640]{2,1,0:T(8,128)(2,1)}, bf16[4,128,640]{2,1,0:T(8,128)(2,1)S(1)}, u32[]{:S(2)}, u32[]{:S(2)}) collective-permute-start(bf16[4,128,640]{2,1,0:T(8,128)(2,1)} %get-tuple-element.55), channel_id=1, source_target_pairs={{0,32},{1,33},{2,34},{3,35},{4,36},{5,37},{6,38},{7,39},{8,40},{9,... | collective-permute-start | bytes 1966088 | tf_op jit(solution)/shard_map/ppermute | solution.py:158
  109.8 67.1 %collective-permute-start.8 = (bf16[4,128,640]{2,1,0:T(8,128)(2,1)}, bf16[4,128,640]{2,1,0:T(8,128)(2,1)S(1)}, u32[]{:S(2)}, u32[]{:S(2)}) collective-permute-start(bf16[4,128,640]{2,1,0:T(8,128)(2,1)} %get-tuple-element.56), channel_id=1, source_target_pairs={{0,36},{1,37},{2,38},{3,39},{4,40},{5,41},{6,42},{7,43},{8,44},{9,... | collective-permute-start | bytes 1966088 | tf_op jit(solution)/shard_map/ppermute | solution.py:158
  109.8 67.2 %collective-permute-start.9 = (bf16[4,128,640]{2,1,0:T(8,128)(2,1)}, bf16[4,128,640]{2,1,0:T(8,128)(2,1)S(1)}, u32[]{:S(2)}, u32[]{:S(2)}) collective-permute-start(bf16[4,128,640]{2,1,0:T(8,128)(2,1)} %get-tuple-element.57), channel_id=1, source_target_pairs={{0,40},{1,41},{2,42},{3,43},{4,44},{5,45},{6,46},{7,47},{8,32},{9,... | collective-permute-start | bytes 1966088 | tf_op jit(solution)/shard_map/ppermute | solution.py:158
  157.0 20.0 %collective-permute-start.10 = (bf16[4,128,640]{2,1,0:T(8,128)(2,1)}, bf16[4,128,640]{2,1,0:T(8,128)(2,1)S(1)}, u32[]{:S(2)}, u32[]{:S(2)}) collective-permute-start(bf16[4,128,640]{2,1,0:T(8,128)(2,1)} %get-tuple-element.58), channel_id=1, source_target_pairs={{0,44},{1,45},{2,46},{3,47},{4,32},{5,33},{6,34},{7,35},{8,36},{9,... | collective-permute-start | bytes 1966088 | tf_op jit(solution)/shard_map/ppermute | solution.py:158
  172.6 59.0 %all-to-all-start = ((bf16[16,128,256]{2,1,0:T(8,128)(2,1)}), bf16[16,128,256]{2,1,0:T(8,128)(2,1)}, u32[]{:S(2)}, u32[]{:S(2)}) async-start(bf16[16,128,256]{2,1,0:T(8,128)(2,1)} %bitcast.8), calls=%async_computation | async-start | bytes 2097152 | tf_op jit(solution)/shard_map/all_to_all | solution.py:425
  182.0 24.5 %collective-permute-start.11 = (bf16[4,128,640]{2,1,0:T(8,128)(2,1)}, bf16[4,128,640]{2,1,0:T(8,128)(2,1)S(1)}, u32[]{:S(2)}, u32[]{:S(2)}) collective-permute-start(bf16[4,128,640]{2,1,0:T(8,128)(2,1)} %get-tuple-element.59), channel_id=1, source_target_pairs={{0,1},{1,2},{2,3},{3,0},{4,5},{5,6},{6,7},{7,4},{8,9},{9,10},{10,1... | collective-permute-start | bytes 1966088 | tf_op jit(solution)/shard_map/ppermute | solution.py:151
  183.8 34.4 %collective-permute-start.12 = (bf16[4,128,640]{2,1,0:T(8,128)(2,1)}, bf16[4,128,640]{2,1,0:T(8,128)(2,1)S(1)}, u32[]{:S(2)}, u32[]{:S(2)}) collective-permute-start(bf16[4,128,640]{2,1,0:T(8,128)(2,1)} %get-tuple-element.60), channel_id=1, source_target_pairs={{0,2},{1,3},{2,0},{3,1},{4,6},{5,7},{6,4},{7,5},{8,10},{9,11},{10,... | collective-permute-start | bytes 1966088 | tf_op jit(solution)/shard_map/ppermute | solution.py:151
  186.5 31.7 %collective-permute-start.13 = (bf16[4,128,640]{2,1,0:T(8,128)(2,1)}, bf16[4,128,640]{2,1,0:T(8,128)(2,1)S(1)}, u32[]{:S(2)}, u32[]{:S(2)}) collective-permute-start(bf16[4,128,640]{2,1,0:T(8,128)(2,1)} %get-tuple-element.61), channel_id=1, source_target_pairs={{0,3},{1,0},{2,1},{3,2},{4,7},{5,4},{6,5},{7,6},{8,11},{9,8},{10,9... | collective-permute-start | bytes 1966088 | tf_op jit(solution)/shard_map/ppermute | solution.py:151
  191.1 40.5 %collective-permute-start.1 = (bf16[4,128,384]{2,1,0:T(8,128)(2,1)}, bf16[4,128,384]{2,1,0:T(8,128)(2,1)S(1)}, u32[]{:S(2)}, u32[]{:S(2)}) collective-permute-start(bf16[4,128,384]{2,1,0:T(8,128)(2,1)} %get-tuple-element.49), channel_id=1, source_target_pairs={{0,4},{1,5},{2,6},{3,7},{4,8},{5,9},{6,10},{7,11},{8,12},{9,13},{1... | collective-permute-start | bytes 1179656 | tf_op jit(solution)/shard_map/ppermute | solution.py:151
  192.7 39.0 %collective-permute-start.2 = (bf16[4,128,384]{2,1,0:T(8,128)(2,1)}, bf16[4,128,384]{2,1,0:T(8,128)(2,1)S(1)}, u32[]{:S(2)}, u32[]{:S(2)}) collective-permute-start(bf16[4,128,384]{2,1,0:T(8,128)(2,1)} %get-tuple-element.50), channel_id=1, source_target_pairs={{0,8},{1,9},{2,10},{3,11},{4,12},{5,13},{6,14},{7,15},{8,0},{9,1},... | collective-permute-start | bytes 1179656 | tf_op jit(solution)/shard_map/ppermute | solution.py:151
  206.6 25.1 %collective-permute-start.3 = (bf16[4,128,384]{2,1,0:T(8,128)(2,1)}, bf16[4,128,384]{2,1,0:T(8,128)(2,1)S(1)}, u32[]{:S(2)}, u32[]{:S(2)}) collective-permute-start(bf16[4,128,384]{2,1,0:T(8,128)(2,1)} %get-tuple-element.51), channel_id=1, source_target_pairs={{0,12},{1,13},{2,14},{3,15},{4,0},{5,1},{6,2},{7,3},{8,4},{9,5},{1... | collective-permute-start | bytes 1179656 | tf_op jit(solution)/shard_map/ppermute | solution.py:151
  222.8 42.2 %collective-permute-start.14 = (bf16[4,128,640]{2,1,0:T(8,128)(2,1)}, bf16[4,128,640]{2,1,0:T(8,128)(2,1)S(1)}, u32[]{:S(2)}, u32[]{:S(2)}) collective-permute-start(bf16[4,128,640]{2,1,0:T(8,128)(2,1)} %edge.2), channel_id=1, source_target_pairs={{0,16},{1,17},{2,18},{3,19},{4,20},{5,21},{6,22},{7,23},{8,24},{9,... | collective-permute-start | bytes 1966088 | tf_op jit(solution)/shard_map/ppermute | solution.py:214
  231.5 63.1 %collective-permute-start.34 = (bf16[16,128,256]{2,1,0:T(8,128)(2,1)}, bf16[16,128,256]{2,1,0:T(8,128)(2,1)}, u32[]{:S(2)}, u32[]{:S(2)}) collective-permute-start(bf16[16,128,256]{2,1,0:T(8,128)(2,1)} %all-to-all-done), channel_id=1, source_target_pairs={{0,32},{32,64},{64,96},{96,128},{128,160},{160,192},{192,224},{224... | collective-permute-start | bytes 3145736 | tf_op jit(solution)/shard_map/ppermute | solution.py:163
  235.0 18.5 %collective-permute-start.4 = (bf16[4,128,384]{2,1,0:T(8,128)(2,1)}, bf16[4,128,384]{2,1,0:T(8,128)(2,1)S(1)}, u32[]{:S(2)}, u32[]{:S(2)}) collective-permute-start(bf16[4,128,384]{2,1,0:T(8,128)(2,1)} %get-tuple-element.52), channel_id=1, source_target_pairs={{0,1},{1,2},{2,3},{3,0},{4,5},{5,6},{6,7},{7,4},{8,9},{9,10},{10,1... | collective-permute-start | bytes 1179656 | tf_op jit(solution)/shard_map/ppermute | solution.py:151
  (41 other events, 329.7 us)
where the time goes:
time: 313 us; the launch traced here: 312 us
  waiting for transfers between devices  156 us (50%)
  starting transfers between devices  73.6 us (24%)
  Pallas kernels  66.7 us (21%)
  local copies, waits for them, and re-layouts  13.7 us (4%)
    ppermute x27, waiting for transfers between devices, routed(): return lax.ppermute(block, 'seq', routes)  109 us
    ppermute x27, starting transfers between devices, routed(): return lax.ppermute(block, 'seq', routes)  49 us
    ppermute x2, waiting for transfers between devices, send_edge(): return lax.ppermute(edge, 'seq', [(i, i + GROUP) for i in range(GROUP)])  47.2 us
    pallas_call x3, Pallas kernels, attention(): pl.pallas_call(functools.partial(attention_kernel, plan), out_shape=[jax....  27.9 us
    ppermute x2, starting transfers between devices, send_edge(): return lax.ppermute(edge, 'seq', [(i, i + GROUP) for i in range(GROUP)])  17.9 us
    pallas_call x4, Pallas kernels, pack(): pl.pallas_call(functools.partial(pack_kernel, tuple(plan), order), out_sh...  13.7 us
    pallas_call x5, Pallas kernels, repack(): pl.pallas_call(functools.partial(repack_kernel, begin), out_shape=[jax.Sh...  12.4 us
    unnamed x58, local copies, waits for them, and re-layouts  11.9 us
  transfers between devices with their start and end apart: 36, of which 16 were waited for; matrix products, arithmetic and copies ran while one was open for 1% of the time, Pallas kernels for 18%

commit v1 on v0

--- a/solution.py
+++ b/solution.py
@@ -22,6 +22,7 @@
 WV = PER * DV
 WKV = WQK + WV
 NEGATIVE = -1e30
+VMEM_LIMIT = 65500 * 1024
 ANY = pl.BlockSpec(memory_space=pl.ANY)
 SMEM = pl.BlockSpec(memory_space=pltpu.SMEM)
 
@@ -94,6 +95,7 @@
             pltpu.SemaphoreType.DMA((SIDE, SIDE, len(parts))),
             pltpu.SemaphoreType.DMA((SIDE,)),
         ],
+        compiler_params=pltpu.CompilerParams(vmem_limit_bytes=VMEM_LIMIT),
         name="pack",
     )(place, *[part[0] for part in parts])
 
@@ -131,6 +133,7 @@
             pltpu.SemaphoreType.DMA((SIDE,)),
             pltpu.SemaphoreType.DMA((count,)),
         ],
+        compiler_params=pltpu.CompilerParams(vmem_limit_bytes=VMEM_LIMIT),
         name="repack",
     )(*arrays)
 
@@ -209,6 +212,7 @@
         in_specs=[SMEM] + [ANY] * len(arrays),
         out_specs=ANY,
         scratch_shapes=[pltpu.VMEM(shape, jnp.bfloat16), pltpu.SemaphoreType.DMA((SIDE,))],
+        compiler_params=pltpu.CompilerParams(vmem_limit_bytes=VMEM_LIMIT),
         name="edge",
     )(place, *arrays)
     return lax.ppermute(edge, "seq", [(i, i + GROUP) for i in range(GROUP)])
@@ -251,6 +255,7 @@
             pltpu.SemaphoreType.DMA((1,)),
         ],
         input_output_aliases={len(arrays) + 1: 0} if extra else {},
+        compiler_params=pltpu.CompilerParams(vmem_limit_bytes=VMEM_LIMIT),
         name="place",
     )(place, *arrays, *extra)
 
@@ -262,7 +267,7 @@
     return start
 
 
-def attend(doc_starts, first_position, queries_in, window, mixed_out, first, last):
+def attend(doc_starts, first_position, queries_in, window, mixed_out, first, last, extras):
     lane = lax.broadcasted_iota(jnp.int32, (BLOCK, LANES), 1)
     sublane = lax.broadcasted_iota(jnp.int32, (BLOCK, LANES), 0)
     column = lax.broadcasted_iota(jnp.int32, (BLOCK, 2 * LANES), 1)
@@ -312,7 +317,7 @@
         start = latest_start(doc_starts, position + sublane)
         back = position - latest_start(doc_starts, position)
         shorter = 0
-        for extra in EXTRA:
+        for extra in extras:
             pl.when((back > shorter) & (back <= extra) | (back == 0) & (shorter == 0))(
                 functools.partial(heads, row, start, BLOCK + extra)
             )
@@ -373,9 +378,13 @@
     border = LONGEST // BLOCK
     first = border if part == "rest" else 0
     last = border if part == "edge" else rows // BLOCK
-    attend(doc_starts, place[2], queries_in, window, mixed_out, first, last)
+    extras = EXTRA[-1:] if part == "edge" else EXTRA
+    attend(doc_starts, place[2], queries_in, window, mixed_out, first, last, extras)
     if order is None:
-        run_copies([pltpu.make_async_copy(mixed_out, targets[0], edge_sems.at[0])])
+        begin = LONGEST if part == "rest" else 0
+        end = LONGEST if part == "edge" else rows
+        span = pl.ds(begin, end - begin)
+        run_copies([pltpu.make_async_copy(mixed_out.at[span], targets[0].at[span], edge_sems.at[0])])
         return
     copies = []
     for first in range(SIDE):
@@ -416,6 +425,7 @@
             pltpu.SemaphoreType.DMA((SIDE,)),
         ],
         input_output_aliases={len(operands) + i: i for i in range(len(whole))},
+        compiler_params=pltpu.CompilerParams(vmem_limit_bytes=VMEM_LIMIT),
         name="attention",
     )(*operands, *whole)
 
@@ -455,16 +465,20 @@
     q_first = list(pack(place, "xy", [(queries, 0, WQK)]))
     kv_first[3], q_first[1] = together(kv_first[3], q_first[1])
     q_first = first_stage(q_first, "xy")
-    q_second = first_stage(pack(place, "yx", [(q_second, 0, WQK)]), "yx")
+    q_second = list(pack(place, "yx", [(q_second, 0, WQK)]))
 
     kv_first = second_stage(kv_first, "xy")
+    kv_first[0][-1], q_second[1] = together(kv_first[0][-1], q_second[1])
+    q_second = first_stage(q_second, "yx")
     kv_second = second_stage(kv_second, "yx")
     edge_first = send_edge(place, *kv_first)
     q_first = second_stage(q_first, "xy")
     edge_second = send_edge(place, *kv_second)
     q_second = second_stage(q_second, "yx")
 
-    (out,) = attention(starts_here, place, q_first, kv_first, edge_first, None)
+    first = (starts_here, place, q_first, kv_first)
+    out = attention(*first, kv_first[0][0], None, "rest")
+    (out,) = attention(*first, edge_first, None, "edge", tuple(out))
     out_first = exchange(out.reshape(GROUP, rows, WV))
     second = (starts_before, place, q_second, kv_second)
     out = attention(*second, kv_second[0][0], "yx", "rest")

time: 313 us -> 296 us (0.946)
  waiting for transfers between devices: 156 us -> 131 us
  starting transfers between devices: 73.6 us -> 86.6 us
  local copies, waits for them, and re-layouts: 13.7 us -> 3.28 us
  Pallas kernels: 66.7 us -> 70.8 us
    ppermute x2, waiting for transfers between devices: 47.2 us -> 32 us  [send_edge(): return lax.ppermute(edge, 'seq', [(i, i + GROUP) for i in range(GROUP)])]
    ppermute x2, starting transfers between devices: 17.9 us -> 31.6 us  [send_edge(): return lax.ppermute(edge, 'seq', [(i, i + GROUP) for i in range(GROUP)])]
    unnamed x58 -> x0, local copies, waits for them, and re-layouts: 11.9 us -> none
    ppermute x27, waiting for transfers between devices: 109 us -> 98.5 us  [routed(): return lax.ppermute(block, 'seq', routes)]
    pallas_call x3 -> x4, Pallas kernels: 27.9 us -> 32.3 us  [attention(): pl.pallas_call(functools.partial(attention_kernel, plan), out_shape=[jax....]
  transfers between devices with their start and end apart: 36 -> 36, of which waited for: 16 -> 15; matrix products, arithmetic and copies ran while one was open for 1% -> 1% of each run, Pallas kernels for 18% -> 23%
where the time goes in v1:
time: 296 us; the launch traced here: 294 us
  waiting for transfers between devices  131 us (44%)
  starting transfers between devices  86.6 us (29%)
  Pallas kernels  70.8 us (24%)
  local copies, waits for them, and re-layouts  3.28 us (1%)
    ppermute x27, waiting for transfers between devices, routed(): return lax.ppermute(block, 'seq', routes)  98.5 us
    ppermute x27, starting transfers between devices, routed(): return lax.ppermute(block, 'seq', routes)  47 us
    pallas_call x4, Pallas kernels, attention(): pl.pallas_call(functools.partial(attention_kernel, plan), out_shape=[jax....  32.3 us
    ppermute x2, waiting for transfers between devices, send_edge(): return lax.ppermute(edge, 'seq', [(i, i + GROUP) for i in range(GROUP)])  32 us
    ppermute x2, starting transfers between devices, send_edge(): return lax.ppermute(edge, 'seq', [(i, i + GROUP) for i in range(GROUP)])  31.6 us
    pallas_call x4, Pallas kernels, pack(): pl.pallas_call(functools.partial(pack_kernel, tuple(plan), order), out_sh...  13.7 us
    pallas_call x5, Pallas kernels, repack(): pl.pallas_call(functools.partial(repack_kernel, begin), out_shape=[jax.Sh...  12.5 us
    pallas_call x2, Pallas kernels, put(): pl.pallas_call(functools.partial(place_kernel, first, table), out_shape=j...  6.9 us
  transfers between devices with their start and end apart: 36, of which 15 were waited for; matrix products, arithmetic and copies ran while one was open for 1% of the time, Pallas kernels for 23%

profile of v1, /device:TPU:32, one launch (start us, length us, event | category | flops | bytes accessed | tf_op | source)
XLA Modules:
  0.0 293.8 jit_solution(3448378534053850649)
XLA Ops:
  3.2 3.7 %pack.5 = (bf16[4,128,640]{2,1,0:T(8,128)(2,1)}, bf16[4,128,640]{2,1,0:T(8,128)(2,1)}, bf16[4,128,640]{2,1,0:T(8,128)(2,1)}, bf16[4,128,640]{2,1,0:T(8,128)(2,1)}) custom-call(s32[3]{0:T(128)} %pad_add_fusion.place, bf16[1,128,12288]{2,1,0:T(8,128)(2,1)} %refs_0_.4, bf16[1,128,8192]{2,1,0:T(8,128)(2,1)} %refs_1_.3), custom_call_target="tpu_custom_call" | custom-call | tf_op jit(solution)/shard_map/pack/pallas_call | solution.py:88
  12.1 13.0 %collective-permute-done.1.refs_1_.refs_8_ = bf16[4,128,640]{2,1,0:T(8,128)(2,1)} collective-permute-done((bf16[4,128,640]{2,1,0:T(8,128)(2,1)}, bf16[4,128,640]{2,1,0:T(8,128)(2,1)}, u32[]{:S(2)}, u32[]{:S(2)}) %collective-permute-start.1) | collective-permute-done | bytes 655392 | tf_op jit(solution)/shard_map/ppermute | solution.py:154
  31.4 8.9 %collective-permute-done.2.refs_2_.refs_9_ = bf16[4,128,640]{2,1,0:T(8,128)(2,1)} collective-permute-done((bf16[4,128,640]{2,1,0:T(8,128)(2,1)}, bf16[4,128,640]{2,1,0:T(8,128)(2,1)}, u32[]{:S(2)}, u32[]{:S(2)}) %collective-permute-start.2) | collective-permute-done | bytes 655392 | tf_op jit(solution)/shard_map/ppermute | solution.py:154
  49.8 3.2 %collective-permute-start.32 = (bf16[4,128,640]{2,1,0:T(8,128)(2,1)}, bf16[4,128,640]{2,1,0:T(8,128)(2,1)}, u32[]{:S(2)}, u32[]{:S(2)}) collective-permute-start(bf16[4,128,640]{2,1,0:T(8,128)(2,1)} %get-tuple-element.93), channel_id=1, source_target_pairs={{0,8},{1,9},{2,10},{3,11},{4,12},{5,13},{6,14},{7,15},{8,0},{9,1},... | collective-permute-start | bytes 1966088 | tf_op jit(solution)/shard_map/ppermute | solution.py:154
  53.0 5.8 %collective-permute-done.27.refs_3_ = bf16[4,128,384]{2,1,0:T(8,128)(2,1)} collective-permute-done((bf16[4,128,384]{2,1,0:T(8,128)(2,1)}, bf16[4,128,384]{2,1,0:T(8,128)(2,1)}, u32[]{:S(2)}, u32[]{:S(2)}) %collective-permute-start.27) | collective-permute-done | bytes 393248 | tf_op jit(solution)/shard_map/ppermute | solution.py:154
  68.4 5.6 %collective-permute-done.32.refs_5_.refs_12_ = bf16[4,128,640]{2,1,0:T(8,128)(2,1)} collective-permute-done((bf16[4,128,640]{2,1,0:T(8,128)(2,1)}, bf16[4,128,640]{2,1,0:T(8,128)(2,1)}, u32[]{:S(2)}, u32[]{:S(2)}) %collective-permute-start.32) | collective-permute-done | bytes 655392 | tf_op jit(solution)/shard_map/ppermute | solution.py:154
  76.7 22.5 %collective-permute-start.33 = (bf16[4,128,640]{2,1,0:T(8,128)(2,1)}, bf16[4,128,640]{2,1,0:T(8,128)(2,1)}, u32[]{:S(2)}, u32[]{:S(2)}) collective-permute-start(bf16[4,128,640]{2,1,0:T(8,128)(2,1)} %edge.3), channel_id=1, source_target_pairs={{0,16},{1,17},{2,18},{3,19},{4,20},{5,21},{6,22},{7,23},{8,24},{9,... | collective-permute-start | bytes 1966088 | tf_op jit(solution)/shard_map/ppermute | solution.py:218
  99.2 3.7 %pack.7 = (bf16[4,128,640]{2,1,0:T(8,128)(2,1)}, bf16[4,128,640]{2,1,0:T(8,128)(2,1)}, bf16[4,128,640]{2,1,0:T(8,128)(2,1)}, bf16[4,128,640]{2,1,0:T(8,128)(2,1)}) custom-call(s32[3]{0:T(128)} %pad_add_fusion.place, bf16[1,128,12288]{2,1,0:T(8,128)(2,1)} %refs_0_.4, bf16[1,128,8192]{2,1,0:T(8,128)(2,1)} %refs_1_.3), custom_call_target="tpu_custom_call" | custom-call | tf_op jit(solution)/shard_map/pack/pallas_call | solution.py:88
  108.7 10.6 %attention.6.refs_15_ = bf16[2048,256]{1,0:T(8,128)(2,1)} custom-call(s32[16]{0:T(128)} %get-tuple-element.95.doc_starts, s32[3]{0:T(128)} %pad_add_fusion.place, bf16[4,128,384]{2,1,0:T(8,128)(2,1)} %get-tuple-element.85.refs_0_, bf16[4,128,384]{2,1,0:T(8,128)(2,1)} %collective-permute-done.25.refs_1_, ...), custom_call_target="tpu_custom_call" | custom-call | tf_op jit(solution)/shard_map/attention/pallas_call | solution.py:415
  119.3 32.0 %collective-permute-done.33.refs_14_ = bf16[4,128,640]{2,1,0:T(8,128)(2,1)} collective-permute-done((bf16[4,128,640]{2,1,0:T(8,128)(2,1)}, bf16[4,128,640]{2,1,0:T(8,128)(2,1)}, u32[]{:S(2)}, u32[]{:S(2)}) %collective-permute-start.33) | collective-permute-done | bytes 655392 | tf_op jit(solution)/shard_map/ppermute | solution.py:218
  151.2 5.8 %attention.7 = bf16[2048,256]{1,0:T(8,128)(2,1)} custom-call(s32[16]{0:T(128)} %get-tuple-element.95.doc_starts, s32[3]{0:T(128)} %pad_add_fusion.place, bf16[4,128,384]{2,1,0:T(8,128)(2,1)} %get-tuple-element.85.refs_0_, bf16[4,128,384]{2,1,0:T(8,128)(2,1)} %collective-permute-done.25.refs_1_, ...), custom_call_target="tpu_custom_call", output_to_operand_aliasing={{}: (17, {})} | custom-call | tf_op jit(solution)/shard_map/attention/pallas_call | solution.py:415
  157.0 4.4 %all-to-all-start = ((bf16[16,128,256]{2,1,0:T(8,128)(2,1)}), bf16[16,128,256]{2,1,0:T(8,128)(2,1)}, u32[]{:S(2)}, u32[]{:S(2)}) async-start(bf16[16,128,256]{2,1,0:T(8,128)(2,1)} %bitcast.8), calls=%async_computation | async-start | bytes 2097152 | tf_op jit(solution)/shard_map/all_to_all | solution.py:435
  174.5 16.4 %collective-permute-done.15.refs_4_.refs_11_ = bf16[4,128,640]{2,1,0:T(8,128)(2,1)} collective-permute-done((bf16[4,128,640]{2,1,0:T(8,128)(2,1)}, bf16[4,128,640]{2,1,0:T(8,128)(2,1)}, u32[]{:S(2)}, u32[]{:S(2)}) %collective-permute-start.15) | collective-permute-done | bytes 655392 | tf_op jit(solution)/shard_map/ppermute | solution.py:154
  190.9 3.2 %collective-permute-start.7 = (bf16[4,128,384]{2,1,0:T(8,128)(2,1)}, bf16[4,128,384]{2,1,0:T(8,128)(2,1)}, u32[]{:S(2)}, u32[]{:S(2)}) collective-permute-start(bf16[4,128,384]{2,1,0:T(8,128)(2,1)} %get-tuple-element.63), channel_id=1, source_target_pairs={{0,12},{1,13},{2,14},{3,15},{4,0},{5,1},{6,2},{7,3},{8,4},{9,5},{1... | collective-permute-start | bytes 1179656 | tf_op jit(solution)/shard_map/ppermute | solution.py:154
  194.0 11.2 %collective-permute-done.16.refs_5_.refs_12_ = bf16[4,128,640]{2,1,0:T(8,128)(2,1)} collective-permute-done((bf16[4,128,640]{2,1,0:T(8,128)(2,1)}, bf16[4,128,640]{2,1,0:T(8,128)(2,1)}, u32[]{:S(2)}, u32[]{:S(2)}) %collective-permute-start.16) | collective-permute-done | bytes 655392 | tf_op jit(solution)/shard_map/ppermute | solution.py:154
  207.9 9.2 %collective-permute-start.18 = (bf16[4,128,640]{2,1,0:T(8,128)(2,1)}, bf16[4,128,640]{2,1,0:T(8,128)(2,1)}, u32[]{:S(2)}, u32[]{:S(2)}) collective-permute-start(bf16[4,128,640]{2,1,0:T(8,128)(2,1)} %edge.2), channel_id=1, source_target_pairs={{0,16},{1,17},{2,18},{3,19},{4,20},{5,21},{6,22},{7,23},{8,24},{9,... | collective-permute-start | bytes 1966088 | tf_op jit(solution)/shard_map/ppermute | solution.py:218
  221.5 3.9 %collective-permute-start.9 = (bf16[4,128,384]{2,1,0:T(8,128)(2,1)}, bf16[4,128,384]{2,1,0:T(8,128)(2,1)}, u32[]{:S(2)}, u32[]{:S(2)}) collective-permute-start(bf16[4,128,384]{2,1,0:T(8,128)(2,1)} %get-tuple-element.65), channel_id=1, source_target_pairs={{0,2},{1,3},{2,0},{3,1},{4,6},{5,7},{6,4},{7,5},{8,10},{9,11},{10,... | collective-permute-start | bytes 1179656 | tf_op jit(solution)/shard_map/ppermute | solution.py:154
  225.4 6.4 %collective-permute-done.10.refs_6_ = bf16[4,128,384]{2,1,0:T(8,128)(2,1)} collective-permute-done((bf16[4,128,384]{2,1,0:T(8,128)(2,1)}, bf16[4,128,384]{2,1,0:T(8,128)(2,1)}, u32[]{:S(2)}, u32[]{:S(2)}) %collective-permute-start.10) | collective-permute-done | bytes 393248 | tf_op jit(solution)/shard_map/ppermute | solution.py:154
  233.3 9.0 %collective-permute-done.9.refs_5_ = bf16[4,128,384]{2,1,0:T(8,128)(2,1)} collective-permute-done((bf16[4,128,384]{2,1,0:T(8,128)(2,1)}, bf16[4,128,384]{2,1,0:T(8,128)(2,1)}, u32[]{:S(2)}, u32[]{:S(2)}) %collective-permute-start.9) | collective-permute-done | bytes 393248 | tf_op jit(solution)/shard_map/ppermute | solution.py:154
  242.3 10.1 %attention.4 = (bf16[4,128,256]{2,1,0:T(8,128)(2,1)}, bf16[4,128,256]{2,1,0:T(8,128)(2,1)}, bf16[4,128,256]{2,1,0:T(8,128)(2,1)}, bf16[4,128,256]{2,1,0:T(8,128)(2,1)}) custom-call(s32[16]{0:T(128)} %get-tuple-element.96.doc_starts, s32[3]{0:T(128)} %pad_add_fusion.place, bf16[4,128,384]{2,1,0:T(8,128)(2,1)} %get-tuple-element.50.refs_0_, ...), custom_call_target="tpu_custom_call" | custom-call | tf_op jit(solution)/shard_map/attention/pallas_call | solution.py:415
  252.5 5.8 %attention.5 = (bf16[4,128,256]{2,1,0:T(8,128)(2,1)}, bf16[4,128,256]{2,1,0:T(8,128)(2,1)}, bf16[4,128,256]{2,1,0:T(8,128)(2,1)}, bf16[4,128,256]{2,1,0:T(8,128)(2,1)}) custom-call(s32[16]{0:T(128)} %get-tuple-element.96.doc_starts, s32[3]{0:T(128)} %pad_add_fusion.place, ...), custom_call_target="tpu_custom_call", output_to_operand_aliasing={{0}: (17, {}), {1}: (18, {}), {2}: (19, {}), {3}: (20, {})} | custom-call | tf_op jit(solution)/shard_map/attention/pallas_call | solution.py:415
  261.8 10.7 %collective-permute-done.19.refs_1_ = bf16[4,128,256]{2,1,0:T(8,128)(2,1)} collective-permute-done((bf16[4,128,256]{2,1,0:T(8,128)(2,1)}, bf16[4,128,256]{2,1,0:T(8,128)(2,1)}, u32[]{:S(2)}, u32[]{:S(2)}) %collective-permute-start.19) | collective-permute-done | bytes 262176 | tf_op jit(solution)/shard_map/ppermute | solution.py:154
  281.7 7.5 %collective-permute-done.22.refs_4_ = bf16[4,128,256]{2,1,0:T(8,128)(2,1)} collective-permute-done((bf16[4,128,256]{2,1,0:T(8,128)(2,1)}, bf16[4,128,256]{2,1,0:T(8,128)(2,1)}, u32[]{:S(2)}, u32[]{:S(2)}) %collective-permute-start.22) | collective-permute-done | bytes 262176 | tf_op jit(solution)/shard_map/ppermute | solution.py:154
  289.8 3.9 %place.3 = bf16[1,128,8192]{2,1,0:T(8,128)(2,1)} custom-call(s32[3]{0:T(128)} %pad_add_fusion.place, bf16[4,128,256]{2,1,0:T(8,128)(2,1)} %get-tuple-element.78.refs_0_, bf16[4,128,256]{2,1,0:T(8,128)(2,1)} %collective-permute-done.19.refs_1_, bf16[4,128,256]{2,1,0:T(8,128)(2,1)} %collective-permute-done.20.refs_2_, ...), custom_call_target="tpu_custom_call", output_to_operand_aliasing={{}: (8, {})} | custom-call | tf_op jit(solution)/shard_map/place/pallas_call | solution.py:247
  (70 shorter events, 77.1 us)
Async XLA Ops:
  2.7 61.7 %collective-permute-start = (bf16[1,128,6144]{2,1,0:T(8,128)(2,1)}, bf16[1,128,6144]{2,1,0:T(8,128)(2,1)}, u32[]{:S(2)}, u32[]{:S(2)}) collective-permute-start(bf16[1,128,6144]{2,1,0:T(8,128)(2,1)} %slice.3), channel_id=1, source_target_pairs={{0,32},{32,64},{64,96},{96,128},{128,160},{160,192},{192,224},{224... | collective-permute-start | bytes 4718600 | tf_op jit(solution)/shard_map/ppermute | solution.py:166
  10.3 30.0 %collective-permute-start.2 = (bf16[4,128,640]{2,1,0:T(8,128)(2,1)}, bf16[4,128,640]{2,1,0:T(8,128)(2,1)}, u32[]{:S(2)}, u32[]{:S(2)}) collective-permute-start(bf16[4,128,640]{2,1,0:T(8,128)(2,1)} %get-tuple-element.54), channel_id=1, source_target_pairs={{0,2},{1,3},{2,0},{3,1},{4,6},{5,7},{6,4},{7,5},{8,10},{9,11},{10,... | collective-permute-start | bytes 1966088 | tf_op jit(solution)/shard_map/ppermute | solution.py:154
  28.3 20.2 %collective-permute-start.25 = (bf16[4,128,384]{2,1,0:T(8,128)(2,1)}, bf16[4,128,384]{2,1,0:T(8,128)(2,1)}, u32[]{:S(2)}, u32[]{:S(2)}) collective-permute-start(bf16[4,128,384]{2,1,0:T(8,128)(2,1)} %get-tuple-element.86), channel_id=1, source_target_pairs={{0,1},{1,2},{2,3},{3,0},{4,5},{5,6},{6,7},{7,4},{8,9},{9,10},{10,1... | collective-permute-start | bytes 1179656 | tf_op jit(solution)/shard_map/ppermute | solution.py:154
  28.7 21.1 %collective-permute-start.26 = (bf16[4,128,384]{2,1,0:T(8,128)(2,1)}, bf16[4,128,384]{2,1,0:T(8,128)(2,1)}, u32[]{:S(2)}, u32[]{:S(2)}) collective-permute-start(bf16[4,128,384]{2,1,0:T(8,128)(2,1)} %get-tuple-element.87), channel_id=1, source_target_pairs={{0,2},{1,3},{2,0},{3,1},{4,6},{5,7},{6,4},{7,5},{8,10},{9,11},{10,... | collective-permute-start | bytes 1179656 | tf_op jit(solution)/shard_map/ppermute | solution.py:154
  48.5 19.9 %collective-permute-start.31 = (bf16[4,128,640]{2,1,0:T(8,128)(2,1)}, bf16[4,128,640]{2,1,0:T(8,128)(2,1)}, u32[]{:S(2)}, u32[]{:S(2)}) collective-permute-start(bf16[4,128,640]{2,1,0:T(8,128)(2,1)} %get-tuple-element.92), channel_id=1, source_target_pairs={{0,4},{1,5},{2,6},{3,7},{4,8},{5,9},{6,10},{7,11},{8,12},{9,13},{1... | collective-permute-start | bytes 1966088 | tf_op jit(solution)/shard_map/ppermute | solution.py:154
  49.8 24.2 %collective-permute-start.32 = (bf16[4,128,640]{2,1,0:T(8,128)(2,1)}, bf16[4,128,640]{2,1,0:T(8,128)(2,1)}, u32[]{:S(2)}, u32[]{:S(2)}) collective-permute-start(bf16[4,128,640]{2,1,0:T(8,128)(2,1)} %get-tuple-element.93), channel_id=1, source_target_pairs={{0,8},{1,9},{2,10},{3,11},{4,12},{5,13},{6,14},{7,15},{8,0},{9,1},... | collective-permute-start | bytes 1966088 | tf_op jit(solution)/shard_map/ppermute | solution.py:154
  61.1 41.8 %collective-permute-start.28 = (bf16[4,128,384]{2,1,0:T(8,128)(2,1)}, bf16[4,128,384]{2,1,0:T(8,128)(2,1)}, u32[]{:S(2)}, u32[]{:S(2)}) collective-permute-start(bf16[4,128,384]{2,1,0:T(8,128)(2,1)} %get-tuple-element.89), channel_id=1, source_target_pairs={{0,4},{1,5},{2,6},{3,7},{4,8},{5,9},{6,10},{7,11},{8,12},{9,13},{1... | collective-permute-start | bytes 1179656 | tf_op jit(solution)/shard_map/ppermute | solution.py:154
  61.2 41.8 %collective-permute-start.29 = (bf16[4,128,384]{2,1,0:T(8,128)(2,1)}, bf16[4,128,384]{2,1,0:T(8,128)(2,1)}, u32[]{:S(2)}, u32[]{:S(2)}) collective-permute-start(bf16[4,128,384]{2,1,0:T(8,128)(2,1)} %get-tuple-element.90), channel_id=1, source_target_pairs={{0,8},{1,9},{2,10},{3,11},{4,12},{5,13},{6,14},{7,15},{8,0},{9,1},... | collective-permute-start | bytes 1179656 | tf_op jit(solution)/shard_map/ppermute | solution.py:154
  64.3 40.3 %collective-permute-start.30 = (bf16[4,128,384]{2,1,0:T(8,128)(2,1)}, bf16[4,128,384]{2,1,0:T(8,128)(2,1)}, u32[]{:S(2)}, u32[]{:S(2)}) collective-permute-start(bf16[4,128,384]{2,1,0:T(8,128)(2,1)} %get-tuple-element.91), channel_id=1, source_target_pairs={{0,12},{1,13},{2,14},{3,15},{4,0},{5,1},{6,2},{7,3},{8,4},{9,5},{1... | collective-permute-start | bytes 1179656 | tf_op jit(solution)/shard_map/ppermute | solution.py:154
  76.7 74.5 %collective-permute-start.33 = (bf16[4,128,640]{2,1,0:T(8,128)(2,1)}, bf16[4,128,640]{2,1,0:T(8,128)(2,1)}, u32[]{:S(2)}, u32[]{:S(2)}) collective-permute-start(bf16[4,128,640]{2,1,0:T(8,128)(2,1)} %edge.3), channel_id=1, source_target_pairs={{0,16},{1,17},{2,18},{3,19},{4,20},{5,21},{6,22},{7,23},{8,24},{9,... | collective-permute-start | bytes 1966088 | tf_op jit(solution)/shard_map/ppermute | solution.py:218
  102.9 58.5 %collective-permute-start.11 = (bf16[4,128,640]{2,1,0:T(8,128)(2,1)}, bf16[4,128,640]{2,1,0:T(8,128)(2,1)}, u32[]{:S(2)}, u32[]{:S(2)}) collective-permute-start(bf16[4,128,640]{2,1,0:T(8,128)(2,1)} %get-tuple-element.67), channel_id=1, source_target_pairs={{0,32},{1,33},{2,34},{3,35},{4,36},{5,37},{6,38},{7,39},{8,40},{9,... | collective-permute-start | bytes 1966088 | tf_op jit(solution)/shard_map/ppermute | solution.py:161
  103.0 58.4 %collective-permute-start.12 = (bf16[4,128,640]{2,1,0:T(8,128)(2,1)}, bf16[4,128,640]{2,1,0:T(8,128)(2,1)}, u32[]{:S(2)}, u32[]{:S(2)}) collective-permute-start(bf16[4,128,640]{2,1,0:T(8,128)(2,1)} %get-tuple-element.68), channel_id=1, source_target_pairs={{0,36},{1,37},{2,38},{3,39},{4,40},{5,41},{6,42},{7,43},{8,44},{9,... | collective-permute-start | bytes 1966088 | tf_op jit(solution)/shard_map/ppermute | solution.py:161
  103.1 58.3 %collective-permute-start.13 = (bf16[4,128,640]{2,1,0:T(8,128)(2,1)}, bf16[4,128,640]{2,1,0:T(8,128)(2,1)}, u32[]{:S(2)}, u32[]{:S(2)}) collective-permute-start(bf16[4,128,640]{2,1,0:T(8,128)(2,1)} %get-tuple-element.69), channel_id=1, source_target_pairs={{0,40},{1,41},{2,42},{3,43},{4,44},{5,45},{6,46},{7,47},{8,32},{9,... | collective-permute-start | bytes 1966088 | tf_op jit(solution)/shard_map/ppermute | solution.py:161
  104.7 56.7 %collective-permute-start.14 = (bf16[4,128,640]{2,1,0:T(8,128)(2,1)}, bf16[4,128,640]{2,1,0:T(8,128)(2,1)}, u32[]{:S(2)}, u32[]{:S(2)}) collective-permute-start(bf16[4,128,640]{2,1,0:T(8,128)(2,1)} %get-tuple-element.70), channel_id=1, source_target_pairs={{0,44},{1,45},{2,46},{3,47},{4,32},{5,33},{6,34},{7,35},{8,36},{9,... | collective-permute-start | bytes 1966088 | tf_op jit(solution)/shard_map/ppermute | solution.py:161
  157.0 60.1 %all-to-all-start = ((bf16[16,128,256]{2,1,0:T(8,128)(2,1)}), bf16[16,128,256]{2,1,0:T(8,128)(2,1)}, u32[]{:S(2)}, u32[]{:S(2)}) async-start(bf16[16,128,256]{2,1,0:T(8,128)(2,1)} %bitcast.8), calls=%async_computation | async-start | bytes 2097152 | tf_op jit(solution)/shard_map/all_to_all | solution.py:435
  164.3 26.6 %collective-permute-start.15 = (bf16[4,128,640]{2,1,0:T(8,128)(2,1)}, bf16[4,128,640]{2,1,0:T(8,128)(2,1)}, u32[]{:S(2)}, u32[]{:S(2)}) collective-permute-start(bf16[4,128,640]{2,1,0:T(8,128)(2,1)} %get-tuple-element.71), channel_id=1, source_target_pairs={{0,1},{1,2},{2,3},{3,0},{4,5},{5,6},{6,7},{7,4},{8,9},{9,10},{10,1... | collective-permute-start | bytes 1966088 | tf_op jit(solution)/shard_map/ppermute | solution.py:154
  166.1 39.1 %collective-permute-start.16 = (bf16[4,128,640]{2,1,0:T(8,128)(2,1)}, bf16[4,128,640]{2,1,0:T(8,128)(2,1)}, u32[]{:S(2)}, u32[]{:S(2)}) collective-permute-start(bf16[4,128,640]{2,1,0:T(8,128)(2,1)} %get-tuple-element.72), channel_id=1, source_target_pairs={{0,2},{1,3},{2,0},{3,1},{4,6},{5,7},{6,4},{7,5},{8,10},{9,11},{10,... | collective-permute-start | bytes 1966088 | tf_op jit(solution)/shard_map/ppermute | solution.py:154
  168.8 36.4 %collective-permute-start.17 = (bf16[4,128,640]{2,1,0:T(8,128)(2,1)}, bf16[4,128,640]{2,1,0:T(8,128)(2,1)}, u32[]{:S(2)}, u32[]{:S(2)}) collective-permute-start(bf16[4,128,640]{2,1,0:T(8,128)(2,1)} %get-tuple-element.73), channel_id=1, source_target_pairs={{0,3},{1,0},{2,1},{3,2},{4,7},{5,4},{6,5},{7,6},{8,11},{9,8},{10,9... | collective-permute-start | bytes 1966088 | tf_op jit(solution)/shard_map/ppermute | solution.py:154
  170.2 46.8 %collective-permute-start.5 = (bf16[4,128,384]{2,1,0:T(8,128)(2,1)}, bf16[4,128,384]{2,1,0:T(8,128)(2,1)}, u32[]{:S(2)}, u32[]{:S(2)}) collective-permute-start(bf16[4,128,384]{2,1,0:T(8,128)(2,1)} %get-tuple-element.61), channel_id=1, source_target_pairs={{0,4},{1,5},{2,6},{3,7},{4,8},{5,9},{6,10},{7,11},{8,12},{9,13},{1... | collective-permute-start | bytes 1179656 | tf_op jit(solution)/shard_map/ppermute | solution.py:154
  171.7 45.4 %collective-permute-start.6 = (bf16[4,128,384]{2,1,0:T(8,128)(2,1)}, bf16[4,128,384]{2,1,0:T(8,128)(2,1)}, u32[]{:S(2)}, u32[]{:S(2)}) collective-permute-start(bf16[4,128,384]{2,1,0:T(8,128)(2,1)} %get-tuple-element.62), channel_id=1, source_target_pairs={{0,8},{1,9},{2,10},{3,11},{4,12},{5,13},{6,14},{7,15},{8,0},{9,1},... | collective-permute-start | bytes 1179656 | tf_op jit(solution)/shard_map/ppermute | solution.py:154
  190.9 26.3 %collective-permute-start.7 = (bf16[4,128,384]{2,1,0:T(8,128)(2,1)}, bf16[4,128,384]{2,1,0:T(8,128)(2,1)}, u32[]{:S(2)}, u32[]{:S(2)}) collective-permute-start(bf16[4,128,384]{2,1,0:T(8,128)(2,1)} %get-tuple-element.63), channel_id=1, source_target_pairs={{0,12},{1,13},{2,14},{3,15},{4,0},{5,1},{6,2},{7,3},{8,4},{9,5},{1... | collective-permute-start | bytes 1179656 | tf_op jit(solution)/shard_map/ppermute | solution.py:154
  207.9 44.6 %collective-permute-start.18 = (bf16[4,128,640]{2,1,0:T(8,128)(2,1)}, bf16[4,128,640]{2,1,0:T(8,128)(2,1)}, u32[]{:S(2)}, u32[]{:S(2)}) collective-permute-start(bf16[4,128,640]{2,1,0:T(8,128)(2,1)} %edge.2), channel_id=1, source_target_pairs={{0,16},{1,17},{2,18},{3,19},{4,20},{5,21},{6,22},{7,23},{8,24},{9,... | collective-permute-start | bytes 1966088 | tf_op jit(solution)/shard_map/ppermute | solution.py:218
  217.1 61.6 %collective-permute-start.34 = (bf16[16,128,256]{2,1,0:T(8,128)(2,1)}, bf16[16,128,256]{2,1,0:T(8,128)(2,1)}, u32[]{:S(2)}, u32[]{:S(2)}) collective-permute-start(bf16[16,128,256]{2,1,0:T(8,128)(2,1)} %all-to-all-done), channel_id=1, source_target_pairs={{0,32},{32,64},{64,96},{96,128},{128,160},{160,192},{192,224},{224... | collective-permute-start | bytes 3145736 | tf_op jit(solution)/shard_map/ppermute | solution.py:166
  221.5 20.8 %collective-permute-start.9 = (bf16[4,128,384]{2,1,0:T(8,128)(2,1)}, bf16[4,128,384]{2,1,0:T(8,128)(2,1)}, u32[]{:S(2)}, u32[]{:S(2)}) collective-permute-start(bf16[4,128,384]{2,1,0:T(8,128)(2,1)} %get-tuple-element.65), channel_id=1, source_target_pairs={{0,2},{1,3},{2,0},{3,1},{4,6},{5,7},{6,4},{7,5},{8,10},{9,11},{10,... | collective-permute-start | bytes 1179656 | tf_op jit(solution)/shard_map/ppermute | solution.py:154
  (12 other events, 177.1 us)
